TPU v7x, 32 devices: a whole 2x2x4 slice. The times are simulated.
32 devices in a mesh: section: 4 (over z), node: 4 (over x, core), local: 2 (over y).
Axes of the slice: x: 2, y: 2, z: 4, core: 2. Of those that a mesh axis runs over, the one named last changes fastest.
Arguments:
- section_inputs: bfloat16 [4, 8, 4, 196, 512], P('section', ('node', 'local')), may hold values from -6 to 6
- grad_in: bfloat16 [4, 8, 196, 512], P('section', ('node', 'local')), may hold values from -6 to 6
- loss_grad: bfloat16 [8, 3, 196, 512], P(('node', 'local')), may hold values from -6 to 6
- w_reduce: bfloat16 [4, 512, 256], P('section'), may hold values from -0.25 to 0.25
- w_spatial: bfloat16 [4, 2304, 256], P('section'), may hold values from -0.125 to 0.125
- w_expand: bfloat16 [4, 256, 512], P('section'), may hold values from -0.375 to 0.375
- err_reduce: bfloat16 [4, 8, 512, 256], P('section', ('node', 'local')), may hold values from -360 to 360
- err_spatial: bfloat16 [4, 8, 2304, 256], P('section', ('node', 'local')), may hold values from -360 to 360
- err_expand: bfloat16 [4, 8, 256, 512], P('section', ('node', 'local')), may hold values from -360 to 360
- prior_reduce: float32 [4, 32, 256], P('section'), may hold values from -6 to 6
- prior_spatial: float32 [4, 32, 256], P('section'), may hold values from -6 to 6
- prior_expand: float32 [4, 32, 512], P('section'), may hold values from -6 to 6
Outputs:
- leaving: bfloat16 [4, 8, 196, 512], P('section', ('node', 'local'))
- basis_reduce: float32 [4, 32, 512], P('section', None, ('node', 'local'))
- basis_spatial: float32 [4, 32, 2304], P('section', None, ('node', 'local'))
- basis_expand: float32 [4, 32, 256], P('section', None, ('node', 'local'))
- right_reduce: float32 [4, 32, 256], P('section', None, ('node', 'local'))
- right_spatial: float32 [4, 32, 256], P('section', None, ('node', 'local'))
- right_expand: float32 [4, 32, 512], P('section', None, ('node', 'local'))
All inputs are finite; a program needn't handle non-finite values.
Results may differ from a plain program's by a relative error of at most 0.0095.
Values may be sent and summed in bfloat16 or wider, within the bound.
No kernel may reach another device: no remote copies, remote signals or barrier semaphores. Data moves between devices by JAX's collectives and lax.ppermute only.
A program may use at most 128 MiB of HBM per device.

v0:
```python
import math
import jax
import jax.numpy as jnp
from jax import lax
from jax.sharding import PartitionSpec as P

SIDE = 14
precise = lax.Precision.HIGHEST


def shifted_2(block, axis, distance):
    devices = range(lax.axis_size(axis))
    route = [(i - distance, i) for i in devices if i - distance in devices]
    return lax.ppermute(block, axis, route)


def silu_slope(values):
    logistic = jax.nn.sigmoid(values)
    return logistic * (1.0 + values * (1.0 - logistic))


def tap_shift(values, row_step, col_step, image_side):
    pixels = values.shape[0]
    offset = row_step * image_side + col_step
    padded = jnp.pad(values, ((image_side + 1, image_side + 1), (0, 0)))
    moved = lax.slice_in_dim(
        padded, image_side + 1 + offset, image_side + 1 + offset + pixels, axis=0
    )
    column = lax.broadcasted_iota(jnp.int32, (pixels, 1), 0) % image_side + col_step
    inside = jnp.logical_and(column >= 0, column < image_side)
    return jnp.where(inside, moved, jnp.zeros_like(moved))


def inner_rows(left_operand, right_operand):
    return lax.dot_general(
        left_operand, right_operand, (((0,), (0,)), ((), ())), preferred_element_type=jnp.float32
    )


def inner_cols(left_operand, right_operand, accuracy=None):
    return lax.dot_general(
        left_operand,
        right_operand,
        (((1,), (1,)), ((), ())),
        precision=accuracy,
        preferred_element_type=jnp.float32,
    )


def block_backward(inputs, upstream, reduce_weight, spatial_weight, expand_weight, image_side):
    channels = reduce_weight.shape[1]
    pre_reduce = jnp.dot(inputs, reduce_weight, preferred_element_type=jnp.float32)
    hidden_one = jax.nn.silu(pre_reduce).astype(jnp.bfloat16)
    shifted = []
    pre_spatial = jnp.zeros((inputs.shape[0], channels), jnp.float32)
    for tap in range(9):
        moved = tap_shift(hidden_one, tap // 3 - 1, tap % 3 - 1, image_side)
        shifted.append(moved)
        pre_spatial = pre_spatial + jnp.dot(
            moved,
            spatial_weight[tap * channels : (tap + 1) * channels],
            preferred_element_type=jnp.float32,
        )
    hidden_two = jax.nn.silu(pre_spatial).astype(jnp.bfloat16)
    back_two = inner_cols(upstream, expand_weight)
    back_spatial = (back_two * silu_slope(pre_spatial)).astype(jnp.bfloat16)
    back_one = jnp.zeros((inputs.shape[0], channels), jnp.float32)
    for tap in range(9):
        tap_term = inner_cols(back_spatial, spatial_weight[tap * channels : (tap + 1) * channels])
        back_one = back_one + tap_shift(tap_term, 1 - tap // 3, 1 - tap % 3, image_side)
    back_reduce = (back_one * silu_slope(pre_reduce)).astype(jnp.bfloat16)
    leaving = (upstream.astype(jnp.float32) + inner_cols(back_reduce, reduce_weight)).astype(
        jnp.bfloat16
    )
    spatial_grad = jnp.concatenate(
        [inner_rows(shifted[tap], back_spatial) for tap in range(9)], axis=0
    )
    gradients = (inner_rows(inputs, back_reduce), spatial_grad, inner_rows(hidden_two, upstream))
    return (leaving, gradients)


def local(
    section_inputs,
    grad_in,
    loss_grad,
    w_reduce,
    w_spatial,
    w_expand,
    err_reduce,
    err_spatial,
    err_expand,
    prior_reduce,
    prior_spatial,
    prior_expand,
):
    image_side = SIDE
    weights = (w_reduce[0], w_spatial[0], w_expand[0])
    last_section = lax.axis_index("section") == lax.axis_size("section") - 1
    upstream = grad_in[0, 0]
    leaving = upstream
    totals = tuple((jnp.zeros(weights[member].shape, jnp.float32) for member in range(3)))
    for tick_index in range(section_inputs.shape[2]):
        if tick_index > 0:
            arrived = shifted_2(leaving, "section", -1)
            upstream = jnp.where(last_section, loss_grad[0, tick_index - 1], arrived)
        leaving, gradients = block_backward(
            section_inputs[0, 0, tick_index],
            upstream,
            weights[0],
            weights[1],
            weights[2],
            image_side,
        )
        totals = tuple((totals[member] + gradients[member] for member in range(3)))
    errors = (err_reduce[0, 0], err_spatial[0, 0], err_expand[0, 0])
    matrices = tuple((totals[member] + errors[member].astype(jnp.float32) for member in range(3)))
    priors = (prior_reduce[0], prior_spatial[0], prior_expand[0])
    factors = tuple((inner_cols(priors[member], matrices[member], precise) for member in range(3)))
    replicas = lax.axis_size(("node", "local"))
    replica_index = lax.axis_index(("node", "local"))
    basis_list = []
    summed = lax.psum((factors[0], factors[1], factors[2]), ("node", "local"))
    partial_rights = []
    for member in range(3):
        triangle = jnp.linalg.cholesky(inner_cols(summed[member], summed[member], precise))
        orthonormal = lax.linalg.triangular_solve(
            triangle, summed[member], left_side=True, lower=True
        )
        slice_width = orthonormal.shape[1] // replicas
        own_rows = lax.dynamic_slice_in_dim(
            orthonormal, replica_index * slice_width, slice_width, 1
        )
        basis_list.append(math.sqrt(orthonormal.shape[1]) * own_rows)
        partial_rights.append(
            jnp.dot(
                orthonormal, matrices[member], precision=precise, preferred_element_type=jnp.float32
            )
        )
    between = (
        lax.psum_scatter(
            partial_rights[0].astype(jnp.bfloat16), "node", scatter_dimension=1, tiled=True
        ).astype(jnp.float32),
        lax.psum_scatter(
            partial_rights[1].astype(jnp.bfloat16), "node", scatter_dimension=1, tiled=True
        ).astype(jnp.float32),
        lax.psum_scatter(
            partial_rights[2].astype(jnp.bfloat16), "node", scatter_dimension=1, tiled=True
        ).astype(jnp.float32),
    )
    rights = (
        lax.psum_scatter(between[0], "local", scatter_dimension=1, tiled=True),
        lax.psum_scatter(between[1], "local", scatter_dimension=1, tiled=True),
        lax.psum_scatter(between[2], "local", scatter_dimension=1, tiled=True),
    )
    right_list = tuple(
        (rights[member] / (replicas * math.sqrt(matrices[member].shape[0])) for member in range(3))
    )
    return (
        leaving[None, None],
        basis_list[0][None],
        basis_list[1][None],
        basis_list[2][None],
        right_list[0][None],
        right_list[1][None],
        right_list[2][None],
    )


def solution(mesh):
    return jax.shard_map(
        local,
        mesh=mesh,
        in_specs=(
            P("section", ("node", "local"), None, None, None),
            P("section", ("node", "local"), None, None),
            P(("node", "local"), None, None, None),
            P("section", None, None),
            P("section", None, None),
            P("section", None, None),
            P("section", ("node", "local"), None, None),
            P("section", ("node", "local"), None, None),
            P("section", ("node", "local"), None, None),
            P("section", None, None),
            P("section", None, None),
            P("section", None, None),
        ),
        out_specs=(
            P("section", ("node", "local"), None, None),
            P("section", None, ("node", "local")),
            P("section", None, ("node", "local")),
            P("section", None, ("node", "local")),
            P("section", None, ("node", "local")),
            P("section", None, ("node", "local")),
            P("section", None, ("node", "local")),
        ),
        check_vma=False,
    )
```

profile of v0, /device:TPU:0, one launch (start us, length us, event | category | flops | bytes accessed | tf_op | source)
XLA Modules:
  0.0 292.2 jit_solution(3530639854416297702)
XLA Ops:
  8.1 4.7 %fusion.439 = (bf16[1,1,1,196,512]{4,2,3,1,0:T(2,128)(2,1)S(1)}, bf16[1,1,1,196,512]{4,2,3,1,0:T(2,128)(2,1)}, bf16[1,1,1,196,512]{4,2,3,1,0:T(2,128)(2,1)}, bf16[1,1,1,196,512]{4,2,3,1,0:T(2,128)(2,1)S(1)}) fusion(bf16[1,1,4,196,512]{4,2,3,1,0:T(4,128)(2,1)} %param.13), kind=kLoop, calls=%fused_computation.670 | loop fusion | bytes 1605632 | tf_op jit(solution)/shard_map/slice | solution.py:107
  18.6 1.3 collective-permute-start
  20.2 2.0 fusion.123
  42.6 1.4 copy-done.4
  44.7 1.8 constant_dynamic-update-slice_fusion.7
  46.5 1.7 constant_dynamic-update-slice_fusion.6
  48.2 1.7 constant_dynamic-update-slice_fusion.5
  49.9 1.7 constant_dynamic-update-slice_fusion.4
  51.6 1.7 constant_dynamic-update-slice_fusion.3
  59.8 1.5 collective-permute-start.1
  64.4 1.2 copy-done.7
  65.9 4.6 %collective-permute-done.1 = bf16[196,512]{1,0:T(8,128)(2,1)S(1)} collective-permute-done((bf16[196,512]{1,0:T(8,128)(2,1)S(1)}, bf16[196,512]{1,0:T(8,128)(2,1)S(1)}, u32[]{:S(2)}, u32[]{:S(2)}) %collective-permute-start.1) | collective-permute-done | bytes 200736 | tf_op jit(solution)/shard_map/ppermute | solution.py:14
  73.6 1.3 collective-permute-start.2
  77.7 1.1 copy-done.9
  79.1 2.6 collective-permute-done.2
  87.4 23.9 %psum.23 = f32[32,256]{1,0:T(8,128)S(1)} all-reduce(f32[32,256]{1,0:T(8,128)S(1)} %convolution_bitcast_fusion.2), channel_id=1, replica_groups=mesh['section'=4,'node'=4,'local'=2] {'node','local'}, use_global_device_ids=true, to_apply=%region_4.6 | all-reduce | flops 8192 | bytes 65536 | tf_op jit(solution)/shard_map/psum | solution.py:122
  111.5 2.9 cholesky.81
  115.7 2.4 custom-call.13
  135.0 3.4 %convolution_bitcast_fusion = f32[32,2304]{1,0:T(8,128)} fusion(bf16[1,1,2304,256]{3,2,1,0:T(8,128)(2,1)S(1)} %copy-done.2, f32[1,1,2304,256]{3,2,1,0:T(8,128)S(1)} %copy-done.6, f32[1,1,2304,256]{3,2,1,0:T(8,128)S(1)} %copy-done.10, f32[1,1,2304,256]{3,2,1,0:T(8,128)S(1)} %copy-done.5, f32[1,1,2304,256]{3,2,1,0:T(8,128)S(1)} %copy-done.8, ...), kind=kOutput, calls=%fused_computation | convolution fusion | flops 229441536 | bytes 10944512 | tf_op jit(solution)/shard_map/dot_general | solution.py:41
  141.8 9.6 %reduce-scatter.29.cloned.1.call-done = f32[64,32]{1,0:T(8,128)} async-done(((f32[128,32]{1,0:T(8,128)}), f32[64,32]{1,0:T(8,128)}) %reduce-scatter.29.cloned.1.call-update) | async-done | bytes 8208
  152.9 44.8 %all-reduce.39.cloned.1.call-done = (f32[32,512]{1,0:T(8,128)}, f32[32,2304]{1,0:T(8,128)}) async-done(((f32[32,512]{1,0:T(8,128)}, f32[32,2304]{1,0:T(8,128)}), (f32[32,512]{1,0:T(8,128)}, f32[32,2304]{1,0:T(8,128)})) %all-reduce.39.cloned.1.call-update) | async-done | bytes 360464 | tf_op jit(solution)/shard_map/psum | solution.py:122
  198.8 1.5 fusion.441
  200.3 2.9 %cholesky.70 = f32[32,32]{1,0:T(8,128)S(1)} custom-call(f32[32,32]{1,0:T(8,128)S(1)} %fusion.327), custom_call_target="Cholesky" | custom-call | tf_op jit(solution)/shard_map/jit(cholesky)/cholesky | solution.py:125
  204.6 2.4 custom-call.12
  207.0 1.4 fusion.325
  208.5 2.9 cholesky.59
  212.8 2.4 custom-call.11
  217.7 5.3 %fusion.48 = bf16[32,256]{1,0:T(8,128)(2,1)S(1)} fusion(f32[32,2304]{1,0:T(8,128)S(1)} %fusion.325, bf16[1,1,2304,256]{3,2,1,0:T(8,128)(2,1)S(1)} %copy-done.2, f32[2304,256]{1,0:T(8,128)} %constant_dynamic-update-slice_fusion.27, f32[2304,256]{1,0:T(8,128)} %copy-done.12, f32[2304,256]{1,0:T(8,128)} %constant_dynamic-update-slice_fusion, ...), kind=kOutput, calls=%fused_computation.98 | convolution fusion | flops 229449728 | bytes 10928128 | tf_op jit(solution)/shard_map/dot_general | solution.py:135
  224.6 12.9 %reduce-scatter.19.cloned.1.call-done = bf16[64,32]{1,0:T(8,128)(2,1)} async-done(((bf16[256,32]{1,0:T(8,128)(2,1)}), bf16[64,32]{1,0:T(8,128)(2,1)}) %reduce-scatter.19.cloned.1.call-update) | async-done | bytes 4112
  239.7 19.6 %reduce-scatter.23.cloned.1.call-done = bf16[64,32]{1,0:T(8,128)(2,1)} async-done(((bf16[256,32]{1,0:T(8,128)(2,1)}), bf16[64,32]{1,0:T(8,128)(2,1)}) %reduce-scatter.23.cloned.1.call-update) | async-done | bytes 4112
  260.8 10.5 %reduce-scatter.21.cloned.1.call-done = f32[32,32]{1,0:T(8,128)} async-done(((f32[64,32]{1,0:T(8,128)}), f32[32,32]{1,0:T(8,128)}) %reduce-scatter.21.cloned.1.call-update) | async-done | bytes 4112
  272.7 10.6 %reduce-scatter.25.cloned.1.call-done = f32[32,32]{1,0:T(8,128)} async-done(((f32[64,32]{1,0:T(8,128)}), f32[32,32]{1,0:T(8,128)}) %reduce-scatter.25.cloned.1.call-update) | async-done | bytes 4112
  (294 shorter events, 85.5 us)
Async XLA Ops:
  8.0 4.8 %copy-start = (bf16[1,512,256]{2,1,0:T(8,128)(2,1)S(1)}, bf16[1,512,256]{2,1,0:T(8,128)(2,1)}, u32[]{:S(2)}) copy-start(bf16[1,512,256]{2,1,0:T(8,128)(2,1)} %param.16) | copy-start | bytes 786436
  8.0 5.0 %copy-start.1 = (bf16[1,2304,256]{2,1,0:T(8,128)(2,1)S(1)}, bf16[1,2304,256]{2,1,0:T(8,128)(2,1)}, u32[]{:S(2)}) copy-start(bf16[1,2304,256]{2,1,0:T(8,128)(2,1)} %param.17) | copy-start | bytes 3538948
  8.0 131.1 %reduce-scatter.27.cloned.1.call-start = ((), (), s32[]{:S(2)}) async-start(), calls=%async_computation.10 | async-start | bytes 163840
  12.8 11.5 %copy-start.15 = (bf16[1,1,1,196,512]{4,2,3,1,0:T(2,128)(2,1)}, bf16[1,1,1,196,512]{4,2,3,1,0:T(2,128)(2,1)S(1)}, u32[]{:S(2)}) copy-start(bf16[1,1,1,196,512]{4,2,3,1,0:T(2,128)(2,1)S(1)} %get-tuple-element.10) | copy-start | bytes 602116
  17.3 2.9 %copy-start.27 = (bf16[1,1,196,512]{3,2,1,0:T(8,128)(2,1)S(1)}, bf16[1,1,196,512]{3,2,1,0:T(8,128)(2,1)}, u32[]{:S(2)}) copy-start(bf16[1,1,196,512]{3,2,1,0:T(8,128)(2,1)} %param.14) | copy-start | bytes 602116
  18.6 37.1 %collective-permute-start = (bf16[196,512]{1,0:T(8,128)(2,1)}, bf16[196,512]{1,0:T(8,128)(2,1)}, u32[]{:S(2)}, u32[]{:S(2)}) collective-permute-start(bf16[196,512]{1,0:T(8,128)(2,1)} %fusion.15), channel_id=1, source_target_pairs={{8,0},{16,8},{24,16},{9,1},{17,9},{25,17},{10,2},{18,10},{26,18},{... | collective-permute-start | bytes 602120 | tf_op jit(solution)/shard_map/ppermute | solution.py:14
  44.0 11.5 %copy-start.22 = (f32[196,256]{1,0:T(8,128)S(1)}, f32[196,256]{1,0:T(8,128)}, u32[]{:S(2)}) copy-start(f32[196,256]{1,0:T(8,128)} %convolution_add_fusion.23) | copy-start | bytes 602116
  44.7 8.6 %copy-start.13 = (f32[256,256]{1,0:T(8,128)S(1)}, f32[256,256]{1,0:T(8,128)}, u32[]{:S(2)}) copy-start(f32[256,256]{1,0:T(8,128)} %get-tuple-element.71) | copy-start | bytes 786436
  44.7 9.3 %copy-start.14 = (f32[256,256]{1,0:T(8,128)S(1)}, f32[256,256]{1,0:T(8,128)}, u32[]{:S(2)}) copy-start(f32[256,256]{1,0:T(8,128)} %get-tuple-element.73) | copy-start | bytes 786436
  44.7 11.0 %copy-start.23 = (bf16[1,3,196,512]{3,2,1,0:T(8,128)(2,1)S(1)}, bf16[1,3,196,512]{3,2,1,0:T(8,128)(2,1)}, u32[]{:S(2)}) copy-start(bf16[1,3,196,512]{3,2,1,0:T(8,128)(2,1)} %param.15) | copy-start | bytes 1806340
  46.5 10.2 %copy-start.34 = (bf16[1,256,512]{2,1,0:T(8,128)(2,1)S(1)}, bf16[1,256,512]{2,1,0:T(8,128)(2,1)}, u32[]{:S(2)}) copy-start(bf16[1,256,512]{2,1,0:T(8,128)(2,1)} %param.18) | copy-start | bytes 786436
  59.8 10.7 %collective-permute-start.1 = (bf16[196,512]{1,0:T(8,128)(2,1)S(1)}, bf16[196,512]{1,0:T(8,128)(2,1)S(1)}, u32[]{:S(2)}, u32[]{:S(2)}) collective-permute-start(bf16[196,512]{1,0:T(8,128)(2,1)S(1)} %add_convert_fusion.2), channel_id=1, source_target_pairs={{8,0},{16,8},{24,16},{9,1},{17,9},{25,17},{10,2},{18,10},{26,18},{... | collective-permute-start | bytes 602120 | tf_op jit(solution)/shard_map/ppermute | solution.py:14
  64.2 6.2 %copy-start.21 = (f32[196,256]{1,0:T(8,128)S(1)}, f32[196,256]{1,0:T(8,128)}, u32[]{:S(2)}) copy-start(f32[196,256]{1,0:T(8,128)} %convolution_add_fusion.14) | copy-start | bytes 602116
  65.6 4.9 %copy-start.11 = (f32[2304,256]{1,0:T(8,128)}, f32[2304,256]{1,0:T(8,128)S(1)}, u32[]{:S(2)}) copy-start(f32[2304,256]{1,0:T(8,128)S(1)} %constant_dynamic-update-slice_fusion.9) | copy-start | bytes 7077892
  73.6 8.1 %collective-permute-start.2 = (bf16[196,512]{1,0:T(8,128)(2,1)S(1)}, bf16[196,512]{1,0:T(8,128)(2,1)S(1)}, u32[]{:S(2)}, u32[]{:S(2)}) collective-permute-start(bf16[196,512]{1,0:T(8,128)(2,1)S(1)} %add_convert_fusion.1), channel_id=1, source_target_pairs={{8,0},{16,8},{24,16},{9,1},{17,9},{25,17},{10,2},{18,10},{26,18},{... | collective-permute-start | bytes 602120 | tf_op jit(solution)/shard_map/ppermute | solution.py:14
  77.5 4.2 %copy-start.28 = (f32[196,256]{1,0:T(8,128)S(1)}, f32[196,256]{1,0:T(8,128)}, u32[]{:S(2)}) copy-start(f32[196,256]{1,0:T(8,128)} %convolution_add_fusion.6) | copy-start | bytes 602116
  78.8 3.8 %copy-start.12 = (f32[2304,256]{1,0:T(8,128)}, f32[2304,256]{1,0:T(8,128)S(1)}, u32[]{:S(2)}) copy-start(f32[2304,256]{1,0:T(8,128)S(1)} %constant_dynamic-update-slice_fusion.18) | copy-start | bytes 7077892
  82.4 2.7 copy-start.35
  119.6 31.8 %reduce-scatter.29.cloned.1.call-start = ((), (), s32[]{:S(2)}) async-start(), calls=%async_computation.11 | async-start | bytes 98304
  120.7 7.9 %copy-start.16 = (bf16[1,1,1,196,512]{4,2,3,1,0:T(2,128)(2,1)S(1)}, bf16[1,1,1,196,512]{4,2,3,1,0:T(2,128)(2,1)}, u32[]{:S(2)}) copy-start(bf16[1,1,1,196,512]{4,2,3,1,0:T(2,128)(2,1)} %copy-done.15) | copy-start | bytes 602116
  121.7 13.3 %copy-start.10 = (f32[1,1,2304,256]{3,2,1,0:T(8,128)S(1)}, f32[1,1,2304,256]{3,2,1,0:T(8,128)}, u32[]{:S(2)}) copy-start(f32[1,1,2304,256]{3,2,1,0:T(8,128)} %copy-done.9) | copy-start | bytes 7077892
  123.7 5.1 %copy-start.32 = (f32[1,32,256]{2,1,0:T(8,128)S(1)}, f32[1,32,256]{2,1,0:T(8,128)}, u32[]{:S(2)}) copy-start(f32[1,32,256]{2,1,0:T(8,128)} %param.22) | copy-start | bytes 98308
  124.7 10.3 %copy-start.8 = (f32[1,1,2304,256]{3,2,1,0:T(8,128)S(1)}, f32[1,1,2304,256]{3,2,1,0:T(8,128)}, u32[]{:S(2)}) copy-start(f32[1,1,2304,256]{3,2,1,0:T(8,128)} %copy-done.7) | copy-start | bytes 7077892
  128.6 6.4 %copy-start.6 = (f32[1,1,2304,256]{3,2,1,0:T(8,128)S(1)}, f32[1,1,2304,256]{3,2,1,0:T(8,128)}, u32[]{:S(2)}) copy-start(f32[1,1,2304,256]{3,2,1,0:T(8,128)} %get-tuple-element.38) | copy-start | bytes 7077892
  128.8 6.2 %copy-start.2 = (bf16[1,1,2304,256]{3,2,1,0:T(8,128)(2,1)S(1)}, bf16[1,1,2304,256]{3,2,1,0:T(8,128)(2,1)}, u32[]{:S(2)}) copy-start(bf16[1,1,2304,256]{3,2,1,0:T(8,128)(2,1)} %param.20) | copy-start | bytes 3538948
  128.8 6.2 %copy-start.5 = (f32[1,1,2304,256]{3,2,1,0:T(8,128)S(1)}, f32[1,1,2304,256]{3,2,1,0:T(8,128)}, u32[]{:S(2)}) copy-start(f32[1,1,2304,256]{3,2,1,0:T(8,128)} %copy-done.4) | copy-start | bytes 7077892
  128.9 6.2 %copy-start.31 = (f32[1,32,256]{2,1,0:T(8,128)S(1)}, f32[1,32,256]{2,1,0:T(8,128)}, u32[]{:S(2)}) copy-start(f32[1,32,256]{2,1,0:T(8,128)} %param.23) | copy-start | bytes 98308
  140.8 56.9 %all-reduce.39.cloned.1.call-start = ((), (), s32[]{:S(2)}) async-start(), calls=%async_computation.12 | async-start | bytes 720896 | tf_op jit(solution)/shard_map/psum | solution.py:122
  141.5 95.9 %reduce-scatter.19.cloned.1.call-start = ((), (), s32[]{:S(2)}) async-start(), calls=%async_computation.6 | async-start | bytes 81920
  217.7 41.6 %reduce-scatter.23.cloned.1.call-start = ((), (), s32[]{:S(2)}) async-start(), calls=%async_computation.8 | async-start | bytes 81920
  223.8 47.5 %reduce-scatter.21.cloned.1.call-start = ((), (), s32[]{:S(2)}) async-start(), calls=%async_computation.7 | async-start | bytes 49152
  238.9 44.4 %reduce-scatter.25.cloned.1.call-start = ((), (), s32[]{:S(2)}) async-start(), calls=%async_computation.9 | async-start | bytes 49152
  (16 other events, 29.9 us)
Sparse Core Ops, SparseCore 0:
  119.7 19.3 reduce-scatter.26
  141.3 10.0 reduce-scatter.28
  217.8 19.5 reduce-scatter.18
  239.7 19.5 reduce-scatter.22
  261.3 9.9 reduce-scatter.20
  273.4 9.9 reduce-scatter.24
Sparse Core Ops, SparseCore 1:
  144.4 53.2 all-reduce.38
where the time goes:
time: 293 us; the launch traced here: 292 us
  waiting for transfers between devices  115 us (39%)
  matrix products  68.9 us (24%)
  local copies, waits for them, and re-layouts  37.5 us (13%)
  other arithmetic  25 us (9%)
  blocking collectives  23.9 us (8%)
  between operations  16.9 us (6%)
  starting transfers between devices  4.56 us (2%)
    unnamed x13, waiting for transfers between devices  63.4 us
    psum x1, waiting for transfers between devices, local(): summed = lax.psum((factors[0], factors[1], factors[2]), ('node', 'local'))  44.8 us
    unnamed x121, local copies, waits for them, and re-layouts  31.1 us
    dot_general x44, matrix products, inner_rows(): lax.dot_general(left_operand, right_operand, (((0,), (0,)), ((), ())), pr...  27 us
    psum x1, blocking collectives, local(): summed = lax.psum((factors[0], factors[1], factors[2]), ('node', 'local'))  23.9 us
    dot_general x50, matrix products, inner_cols(): lax.dot_general(left_operand, right_operand, (((1,), (1,)), ((), ())), pr...  19.7 us
    another operation x9, other arithmetic, local(): jnp.linalg.cholesky(inner_cols(summed[member], summed[member], precise))  10.8 us
    dot_general x36, matrix products, block_backward(): jnp.dot(moved, spatial_weight[tap * channels:(tap + 1) * channels], prefe...  10.2 us
  transfers between devices with their start and end apart: 10, of which 8 were waited for; matrix products, arithmetic and copies ran while one was open for 25% of the time, Pallas kernels for 0%

commit v1 on v0

--- a/solution.py
+++ b/solution.py
@@ -119,7 +119,7 @@
     replicas = lax.axis_size(("node", "local"))
     replica_index = lax.axis_index(("node", "local"))
     basis_list = []
-    summed = lax.psum((factors[0], factors[1], factors[2]), ("node", "local"))
+    summed = lax.psum(lax.psum((factors[0], factors[1], factors[2]), "local"), "node")
     partial_rights = []
     for member in range(3):
         triangle = jnp.linalg.cholesky(inner_cols(summed[member], summed[member], precise))

time: 293 us -> 305 us (1.041)
  waiting for transfers between devices: 115 us -> 130 us
  blocking collectives: 23.9 us -> 18.5 us
  matrix products: 68.9 us -> 74.1 us
    psum x1 -> x2, waiting for transfers between devices: 44.8 us -> 61 us  [the longest x1 34.3 us: local(): lax.psum(lax.psum((factors[0], factors[1], factors[2]), 'local'), 'node')]
    dot_general x50, matrix products: 19.7 us -> 25.2 us  [inner_cols(): lax.dot_general(left_operand, right_operand, (((1,), (1,)), ((), ())), pr...]
    psum x1 -> x2, blocking collectives: 23.9 us -> 18.5 us  [the longest x1 10.3 us: local(): lax.psum(lax.psum((factors[0], factors[1], factors[2]), 'local'), 'node')]
    unnamed x13 -> x14, waiting for transfers between devices: 63.4 us -> 61.9 us
    unnamed x121 -> x151, local copies, waits for them, and re-layouts: 31.1 us -> 30.2 us
  transfers between devices with their start and end apart: 10 -> 11, of which waited for: 8 -> 10; matrix products, arithmetic and copies ran while one was open for 25% -> 24% of each run, Pallas kernels for 0% -> 0%
where the time goes in v1:
time: 305 us; the launch traced here: 304 us
  waiting for transfers between devices  130 us (43%)
  matrix products  74.1 us (24%)
  local copies, waits for them, and re-layouts  36.5 us (12%)
  other arithmetic  25 us (8%)
  blocking collectives  18.5 us (6%)
  between operations  15.6 us (5%)
  starting transfers between devices  4.59 us (2%)
    unnamed x14, waiting for transfers between devices  61.9 us
    psum x1, waiting for transfers between devices, local(): lax.psum(lax.psum((factors[0], factors[1], factors[2]), 'local'), 'node')  34.3 us
    unnamed x151, local copies, waits for them, and re-layouts  30.2 us
    psum x1, waiting for transfers between devices, local(): lax.psum((factors[0], factors[1], factors[2]), 'local')  26.6 us
    dot_general x44, matrix products, inner_rows(): lax.dot_general(left_operand, right_operand, (((0,), (0,)), ((), ())), pr...  26.3 us
    dot_general x50, matrix products, inner_cols(): lax.dot_general(left_operand, right_operand, (((1,), (1,)), ((), ())), pr...  25.2 us
    another operation x9, other arithmetic, local(): jnp.linalg.cholesky(inner_cols(summed[member], summed[member], precise))  10.8 us
    psum x1, blocking collectives, local(): lax.psum(lax.psum((factors[0], factors[1], factors[2]), 'local'), 'node')  10.3 us
  transfers between devices with their start and end apart: 11, of which 10 were waited for; matrix products, arithmetic and copies ran while one was open for 24% of the time, Pallas kernels for 0%

profile of v1, /device:TPU:0, one launch (start us, length us, event | category | flops | bytes accessed | tf_op | source)
XLA Modules:
  0.0 304.4 jit_solution(2854002450172380678)
XLA Ops:
  7.3 4.6 %fusion.439 = (bf16[1,1,1,196,512]{4,2,3,1,0:T(2,128)(2,1)}, bf16[1,1,1,196,512]{4,2,3,1,0:T(2,128)(2,1)}, bf16[1,1,1,196,512]{4,2,3,1,0:T(2,128)(2,1)}, bf16[1,1,1,196,512]{4,2,3,1,0:T(2,128)(2,1)S(1)}) fusion(bf16[1,1,4,196,512]{4,2,3,1,0:T(4,128)(2,1)} %param.13), kind=kLoop, calls=%fused_computation.670 | loop fusion | bytes 1605632 | tf_op jit(solution)/shard_map/slice | solution.py:107
  17.7 1.3 collective-permute-start
  21.6 1.9 multiply_convert_fusion.4
  40.1 1.4 copy-done.4
  42.3 1.8 constant_dynamic-update-slice_fusion.7
  44.0 1.7 constant_dynamic-update-slice_fusion.6
  45.8 1.7 constant_dynamic-update-slice_fusion.5
  47.5 1.7 constant_dynamic-update-slice_fusion.4
  49.1 1.7 constant_dynamic-update-slice_fusion.3
  57.3 1.5 collective-permute-start.1
  63.3 4.6 %collective-permute-done.1 = bf16[196,512]{1,0:T(8,128)(2,1)S(1)} collective-permute-done((bf16[196,512]{1,0:T(8,128)(2,1)S(1)}, bf16[196,512]{1,0:T(8,128)(2,1)S(1)}, u32[]{:S(2)}, u32[]{:S(2)}) %collective-permute-start.1) | collective-permute-done | bytes 200736 | tf_op jit(solution)/shard_map/ppermute | solution.py:14
  71.1 1.3 collective-permute-start.2
  76.6 2.6 collective-permute-done.2
  89.1 8.2 %psum.46 = f32[32,256]{1,0:T(8,128)S(1)} all-reduce(f32[32,256]{1,0:T(8,128)S(1)} %convolution_bitcast_fusion.2), channel_id=1, replica_groups=mesh['section'=4,'node'=4,'local'=2] {'local'}, use_global_device_ids=true, to_apply=%region_6.8 | all-reduce | flops 8192 | bytes 65536 | tf_op jit(solution)/shard_map/psum | solution.py:122
  97.3 10.3 %psum.47 = f32[32,256]{1,0:T(8,128)S(1)} all-reduce(f32[32,256]{1,0:T(8,128)S(1)} %psum.46), channel_id=1, replica_groups=mesh['section'=4,'node'=4,'local'=2] {'node'}, use_global_device_ids=true, to_apply=%region_7.9 | all-reduce | flops 8192 | bytes 65536 | tf_op jit(solution)/shard_map/psum | solution.py:122
  107.8 2.9 cholesky.81
  112.1 2.4 custom-call.13
  130.7 3.3 %convolution_bitcast_fusion = f32[32,2304]{1,0:T(8,128)} fusion(bf16[1,1,2304,256]{3,2,1,0:T(8,128)(2,1)S(1)} %copy-done.2, f32[1,1,2304,256]{3,2,1,0:T(8,128)S(1)} %copy-done.6, f32[1,1,2304,256]{3,2,1,0:T(8,128)S(1)} %copy-done.10, f32[1,1,2304,256]{3,2,1,0:T(8,128)S(1)} %copy-done.5, f32[1,1,2304,256]{3,2,1,0:T(8,128)S(1)} %copy-done.8, ...), kind=kOutput, calls=%fused_computation | convolution fusion | flops 229441536 | bytes 10944512 | tf_op jit(solution)/shard_map/dot_general | solution.py:41
  140.5 7.2 %reduce-scatter.29.cloned.1.call-done = f32[64,32]{1,0:T(8,128)} async-done(((f32[128,32]{1,0:T(8,128)}), f32[64,32]{1,0:T(8,128)}) %reduce-scatter.29.cloned.1.call-update) | async-done | bytes 8208
  148.5 26.6 %all-reduce.43.cloned.1.call-done = (f32[32,512]{1,0:T(8,128)}, f32[32,2304]{1,0:T(8,128)}) async-done(((f32[32,512]{1,0:T(8,128)}, f32[32,2304]{1,0:T(8,128)}), (f32[32,512]{1,0:T(8,128)}, f32[32,2304]{1,0:T(8,128)})) %all-reduce.43.cloned.1.call-update) | async-done | bytes 360464 | tf_op jit(solution)/shard_map/psum | solution.py:122
  175.9 34.3 %all-reduce.41.cloned.1.call-done = (f32[32,512]{1,0:T(8,128)}, f32[32,2304]{1,0:T(8,128)}) async-done(((f32[32,512]{1,0:T(8,128)}, f32[32,2304]{1,0:T(8,128)}), (f32[32,512]{1,0:T(8,128)}, f32[32,2304]{1,0:T(8,128)})) %all-reduce.41.cloned.1.call-update) | async-done | bytes 360464 | tf_op jit(solution)/shard_map/psum | solution.py:122
  211.3 1.5 fusion.441
  212.9 2.9 cholesky.70
  217.1 2.4 custom-call.12
  219.5 1.4 fusion.325
  221.1 2.9 cholesky.59
  225.3 2.4 custom-call.11
  230.2 5.3 %fusion.48 = bf16[32,256]{1,0:T(8,128)(2,1)S(1)} fusion(f32[32,2304]{1,0:T(8,128)S(1)} %fusion.325, bf16[1,1,2304,256]{3,2,1,0:T(8,128)(2,1)S(1)} %copy-done.2, f32[2304,256]{1,0:T(8,128)} %constant_dynamic-update-slice_fusion.27, f32[2304,256]{1,0:T(8,128)} %copy-done.12, f32[2304,256]{1,0:T(8,128)} %constant_dynamic-update-slice_fusion, ...), kind=kOutput, calls=%fused_computation.98 | convolution fusion | flops 229449728 | bytes 10928128 | tf_op jit(solution)/shard_map/dot_general | solution.py:135
  237.1 12.8 %reduce-scatter.19.cloned.1.call-done = bf16[64,32]{1,0:T(8,128)(2,1)} async-done(((bf16[256,32]{1,0:T(8,128)(2,1)}), bf16[64,32]{1,0:T(8,128)(2,1)}) %reduce-scatter.19.cloned.1.call-update) | async-done | bytes 4112
  252.2 19.6 %reduce-scatter.23.cloned.1.call-done = bf16[64,32]{1,0:T(8,128)(2,1)} async-done(((bf16[256,32]{1,0:T(8,128)(2,1)}), bf16[64,32]{1,0:T(8,128)(2,1)}) %reduce-scatter.23.cloned.1.call-update) | async-done | bytes 4112
  273.3 10.7 %reduce-scatter.21.cloned.1.call-done = f32[32,32]{1,0:T(8,128)} async-done(((f32[64,32]{1,0:T(8,128)}), f32[32,32]{1,0:T(8,128)}) %reduce-scatter.21.cloned.1.call-update) | async-done | bytes 4112
  285.3 10.8 %reduce-scatter.25.cloned.1.call-done = f32[32,32]{1,0:T(8,128)} async-done(((f32[64,32]{1,0:T(8,128)}), f32[32,32]{1,0:T(8,128)}) %reduce-scatter.25.cloned.1.call-update) | async-done | bytes 4112
  (328 shorter events, 93.0 us)
Async XLA Ops:
  7.2 128.3 %reduce-scatter.27.cloned.1.call-start = ((), (), s32[]{:S(2)}) async-start(), calls=%async_computation.10 | async-start | bytes 163840
  17.7 35.5 %collective-permute-start = (bf16[196,512]{1,0:T(8,128)(2,1)}, bf16[196,512]{1,0:T(8,128)(2,1)}, u32[]{:S(2)}, u32[]{:S(2)}) collective-permute-start(bf16[196,512]{1,0:T(8,128)(2,1)} %fusion.15), channel_id=1, source_target_pairs={{8,0},{16,8},{24,16},{9,1},{17,9},{25,17},{10,2},{18,10},{26,18},{... | collective-permute-start | bytes 602120 | tf_op jit(solution)/shard_map/ppermute | solution.py:14
  29.2 38.8 %copy-start.22 = (f32[196,256]{1,0:T(8,128)}, f32[196,256]{1,0:T(8,128)S(1)}, u32[]{:S(2)}) copy-start(f32[196,256]{1,0:T(8,128)S(1)} %convolution_add_fusion.14) | copy-start | bytes 602116
  41.5 11.5 %copy-start.24 = (f32[196,256]{1,0:T(8,128)S(1)}, f32[196,256]{1,0:T(8,128)}, u32[]{:S(2)}) copy-start(f32[196,256]{1,0:T(8,128)} %convolution_add_fusion.23) | copy-start | bytes 602116
  42.3 8.5 %copy-start.15 = (f32[256,256]{1,0:T(8,128)S(1)}, f32[256,256]{1,0:T(8,128)}, u32[]{:S(2)}) copy-start(f32[256,256]{1,0:T(8,128)} %get-tuple-element.73) | copy-start | bytes 786436
  42.3 9.3 %copy-start.16 = (f32[256,256]{1,0:T(8,128)S(1)}, f32[256,256]{1,0:T(8,128)}, u32[]{:S(2)}) copy-start(f32[256,256]{1,0:T(8,128)} %get-tuple-element.75) | copy-start | bytes 786436
  42.3 11.0 %copy-start.27 = (bf16[1,3,196,512]{3,2,1,0:T(8,128)(2,1)S(1)}, bf16[1,3,196,512]{3,2,1,0:T(8,128)(2,1)}, u32[]{:S(2)}) copy-start(bf16[1,3,196,512]{3,2,1,0:T(8,128)(2,1)} %param.15) | copy-start | bytes 1806340
  44.0 10.2 %copy-start.49 = (bf16[1,256,512]{2,1,0:T(8,128)(2,1)S(1)}, bf16[1,256,512]{2,1,0:T(8,128)(2,1)}, u32[]{:S(2)}) copy-start(bf16[1,256,512]{2,1,0:T(8,128)(2,1)} %param.18) | copy-start | bytes 786436
  57.3 10.7 %collective-permute-start.1 = (bf16[196,512]{1,0:T(8,128)(2,1)S(1)}, bf16[196,512]{1,0:T(8,128)(2,1)S(1)}, u32[]{:S(2)}, u32[]{:S(2)}) collective-permute-start(bf16[196,512]{1,0:T(8,128)(2,1)S(1)} %add_convert_fusion.2), channel_id=1, source_target_pairs={{8,0},{16,8},{24,16},{9,1},{17,9},{25,17},{10,2},{18,10},{26,18},{... | collective-permute-start | bytes 602120 | tf_op jit(solution)/shard_map/ppermute | solution.py:14
  71.1 8.1 %collective-permute-start.2 = (bf16[196,512]{1,0:T(8,128)(2,1)S(1)}, bf16[196,512]{1,0:T(8,128)(2,1)S(1)}, u32[]{:S(2)}, u32[]{:S(2)}) collective-permute-start(bf16[196,512]{1,0:T(8,128)(2,1)S(1)} %add_convert_fusion.1), channel_id=1, source_target_pairs={{8,0},{16,8},{24,16},{9,1},{17,9},{25,17},{10,2},{18,10},{26,18},{... | collective-permute-start | bytes 602120 | tf_op jit(solution)/shard_map/ppermute | solution.py:14
  79.2 7.5 %copy-start.25 = (bf16[196,512]{1,0:T(8,128)(2,1)}, bf16[196,512]{1,0:T(8,128)(2,1)S(1)}, u32[]{:S(2)}) copy-start(bf16[196,512]{1,0:T(8,128)(2,1)S(1)} %bitcast_select_fusion.2) | copy-start | bytes 602116
  81.3 6.8 %copy-start.31 = (bf16[1,1,256,512]{3,2,1,0:T(8,128)(2,1)S(1)}, bf16[1,1,256,512]{3,2,1,0:T(8,128)(2,1)}, u32[]{:S(2)}) copy-start(bf16[1,1,256,512]{3,2,1,0:T(8,128)(2,1)} %param.21) | copy-start | bytes 786436
  116.0 31.7 %reduce-scatter.29.cloned.1.call-start = ((), (), s32[]{:S(2)}) async-start(), calls=%async_computation.11 | async-start | bytes 98304
  118.1 7.0 %copy-start.37 = (f32[196,256]{1,0:T(8,128)S(1)}, f32[196,256]{1,0:T(8,128)}, u32[]{:S(2)}) copy-start(f32[196,256]{1,0:T(8,128)} %fusion.126) | copy-start | bytes 602116
  118.1 7.0 %copy-start.38 = (f32[196,256]{1,0:T(8,128)S(1)}, f32[196,256]{1,0:T(8,128)}, u32[]{:S(2)}) copy-start(f32[196,256]{1,0:T(8,128)} %fusion.138) | copy-start | bytes 602116
  118.1 7.0 %copy-start.39 = (f32[196,256]{1,0:T(8,128)S(1)}, f32[196,256]{1,0:T(8,128)}, u32[]{:S(2)}) copy-start(f32[196,256]{1,0:T(8,128)} %fusion.150) | copy-start | bytes 602116
  118.1 7.0 %copy-start.40 = (f32[196,256]{1,0:T(8,128)S(1)}, f32[196,256]{1,0:T(8,128)}, u32[]{:S(2)}) copy-start(f32[196,256]{1,0:T(8,128)} %fusion.162) | copy-start | bytes 602116
  118.1 7.0 %copy-start.41 = (f32[196,256]{1,0:T(8,128)S(1)}, f32[196,256]{1,0:T(8,128)}, u32[]{:S(2)}) copy-start(f32[196,256]{1,0:T(8,128)} %fusion.182) | copy-start | bytes 602116
  118.1 7.0 %copy-start.42 = (f32[196,256]{1,0:T(8,128)S(1)}, f32[196,256]{1,0:T(8,128)}, u32[]{:S(2)}) copy-start(f32[196,256]{1,0:T(8,128)} %fusion.194) | copy-start | bytes 602116
  118.1 7.0 %copy-start.43 = (f32[196,256]{1,0:T(8,128)S(1)}, f32[196,256]{1,0:T(8,128)}, u32[]{:S(2)}) copy-start(f32[196,256]{1,0:T(8,128)} %fusion.206) | copy-start | bytes 602116
  118.1 7.0 %copy-start.44 = (f32[196,256]{1,0:T(8,128)S(1)}, f32[196,256]{1,0:T(8,128)}, u32[]{:S(2)}) copy-start(f32[196,256]{1,0:T(8,128)} %fusion.218) | copy-start | bytes 602116
  118.1 7.0 %copy-start.50 = (f32[196,256]{1,0:T(8,128)S(1)}, f32[196,256]{1,0:T(8,128)}, u32[]{:S(2)}) copy-start(f32[196,256]{1,0:T(8,128)} %get-tuple-element.23) | copy-start | bytes 602116
  120.2 10.4 %copy-start.46 = (f32[1,32,256]{2,1,0:T(8,128)S(1)}, f32[1,32,256]{2,1,0:T(8,128)}, u32[]{:S(2)}) copy-start(f32[1,32,256]{2,1,0:T(8,128)} %param.23) | copy-start | bytes 98308
  121.2 9.4 %copy-start.10 = (f32[1,1,2304,256]{3,2,1,0:T(8,128)S(1)}, f32[1,1,2304,256]{3,2,1,0:T(8,128)}, u32[]{:S(2)}) copy-start(f32[1,1,2304,256]{3,2,1,0:T(8,128)} %copy-done.9) | copy-start | bytes 7077892
  130.7 8.9 %copy-start.26 = (bf16[196,512]{1,0:T(8,128)(2,1)S(1)}, bf16[196,512]{1,0:T(8,128)(2,1)}, u32[]{:S(2)}) copy-start(bf16[196,512]{1,0:T(8,128)(2,1)} %copy-done.25) | copy-start | bytes 602116
  130.7 8.9 %copy-start.30 = (bf16[196,256]{1,0:T(8,128)(2,1)S(1)}, bf16[196,256]{1,0:T(8,128)(2,1)}, u32[]{:S(2)}) copy-start(bf16[196,256]{1,0:T(8,128)(2,1)} %copy-done.29) | copy-start | bytes 301060
  137.1 38.1 %all-reduce.43.cloned.1.call-start = ((), (), s32[]{:S(2)}) async-start(), calls=%async_computation.13 | async-start | bytes 720896 | tf_op jit(solution)/shard_map/psum | solution.py:122
  137.9 72.3 %all-reduce.41.cloned.1.call-start = ((), (), s32[]{:S(2)}) async-start(), calls=%async_computation.12 | async-start | bytes 720896 | tf_op jit(solution)/shard_map/psum | solution.py:122
  175.2 74.7 %reduce-scatter.19.cloned.1.call-start = ((), (), s32[]{:S(2)}) async-start(), calls=%async_computation.6 | async-start | bytes 81920
  230.2 41.6 %reduce-scatter.23.cloned.1.call-start = ((), (), s32[]{:S(2)}) async-start(), calls=%async_computation.8 | async-start | bytes 81920
  236.3 47.6 %reduce-scatter.21.cloned.1.call-start = ((), (), s32[]{:S(2)}) async-start(), calls=%async_computation.7 | async-start | bytes 49152
  251.4 44.7 %reduce-scatter.25.cloned.1.call-start = ((), (), s32[]{:S(2)}) async-start(), calls=%async_computation.9 | async-start | bytes 49152
  (32 other events, 111.9 us)
Sparse Core Ops, SparseCore 0:
  116.1 19.3 reduce-scatter.26
  137.7 10.0 reduce-scatter.28
  150.0 25.0 all-reduce.42
  177.4 32.7 all-reduce.40
  230.3 19.5 reduce-scatter.18
  252.2 19.5 reduce-scatter.22
  273.9 9.9 reduce-scatter.20
  286.1 9.9 reduce-scatter.24
